TPU v7x, 512 devices: a whole 4x8x8 slice. The times are simulated.
512 devices in a mesh: seq: 64 (over z_hi, y, core), grp: 8 (over x, z_lo).
Axes of the slice: x: 4, y: 8, z: 8 (z_hi: 4, z_lo: 2; z = z_hi * 2 + z_lo), core: 2. Of those that a mesh axis runs over, the one named last changes fastest.
Arguments:
- embeddings: bfloat16 [1536, 32768], P('grp', 'seq'), may hold values from -6 to 6
- hilbert_order: int32 [32768], P('seq'), may hold values from 0 to 32767, as said below
- cotangent: bfloat16 [1536, 32768], P('grp', 'seq'), may hold values from -6 to 6
- first_conv_weight: bfloat16 [8, 110592], P('grp'), may hold values from -0.25 to 0.25
- first_pointwise_weight: bfloat16 [1536, 1536], P('grp'), may hold values from -0.21875 to 0.21875
- second_conv_weight: bfloat16 [8, 110592], P('grp'), may hold values from -0.25 to 0.25
- second_pointwise_weight: bfloat16 [1536, 1536], P('grp'), may hold values from -0.21875 to 0.21875
Outputs:
- emb_grad: bfloat16 [1536, 32768], P('grp', 'seq')
- first_conv_gradient: bfloat16 [8, 110592], P('grp')
- first_pointwise_gradient: bfloat16 [1536, 1536], P('grp')
- second_conv_gradient: bfloat16 [8, 110592], P('grp')
- second_pointwise_gradient: bfloat16 [1536, 1536], P('grp')
Inputs may be any that keep to these rules, and one draw needn't show every extreme that they name: `hilbert_order`: every aligned block of 512 positions holds each patch index of that same block exactly once.
All inputs are finite; a program needn't handle non-finite values.
Results may differ from a plain program's by a relative error of at most 0.018.
Values may be sent and summed in bfloat16 or wider, within the bound.
No kernel may reach another device: no remote copies, remote signals or barrier semaphores. Data moves between devices by JAX's collectives and lax.ppermute only.
A program may use at most 64 MiB of HBM per device.

v0:
```python
import jax
import jax.numpy as jnp
from jax import lax
from jax.sharding import PartitionSpec as P

CG = 192


def passed_along(block, axis, distance):
    devices = range(lax.axis_size(axis))
    route = [(i - distance, i) for i in devices if i - distance in devices]
    return lax.ppermute(block, axis, route)


def shard_taps(inputs, shift_by):
    earlier = passed_along(inputs, "seq", shift_by)
    following = passed_along(inputs, "seq", -shift_by)
    return (earlier, inputs, following)


def grad_taps(grad_pre, shift_by):
    following = passed_along(grad_pre, "seq", -shift_by)
    earlier = passed_along(grad_pre, "seq", shift_by)
    return (following, grad_pre, earlier)


def tap_weights(conv_weight, tap):
    groups_here = conv_weight.shape[0]
    return conv_weight.reshape(groups_here, 3, CG, CG)[:, tap]


def group_apply(values, weight_tap):
    channels, col_count = values.shape
    groups_here = channels // CG
    return jnp.einsum(
        "git,gio->got",
        values.reshape(groups_here, CG, col_count),
        weight_tap,
        preferred_element_type=jnp.float32,
    ).reshape(channels, col_count)


def group_back(grads, weight_tap):
    channels, col_count = grads.shape
    groups_here = channels // CG
    return jnp.einsum(
        "got,gio->git",
        grads.reshape(groups_here, CG, col_count),
        weight_tap,
        preferred_element_type=jnp.float32,
    ).reshape(channels, col_count)


def group_grad(values, grads):
    channels, col_count = values.shape
    groups_here = channels // CG
    return jnp.einsum(
        "git,got->gio",
        values.reshape(groups_here, CG, col_count),
        grads.reshape(groups_here, CG, col_count),
        preferred_element_type=jnp.float32,
    )


def block_forward_step(inputs, conv_weight, shift_by):
    tap_set = shard_taps(inputs, shift_by)
    hidden = (
        group_apply(tap_set[0], tap_weights(conv_weight, 0))
        + group_apply(tap_set[1], tap_weights(conv_weight, 1))
        + group_apply(tap_set[2], tap_weights(conv_weight, 2))
    )
    activated = jax.nn.silu(hidden).astype(jnp.bfloat16)
    gathered = lax.all_gather(activated, "grp", axis=0, tiled=True)
    return (tap_set, hidden, gathered)


def block_backward_step(
    grad_out, tap_set, hidden, gathered, conv_weight, pointwise, shift_by, gradient_scale
):
    shard_width, col_count = grad_out.shape
    groups_here = conv_weight.shape[0]
    point_grad = lax.dot_general(
        grad_out, gathered, (((1,), (1,)), ((), ())), preferred_element_type=jnp.float32
    )
    weight_rows = lax.all_to_all(pointwise, "grp", split_axis=1, concat_axis=0, tiled=True)
    block_in = lax.all_gather(grad_out, "grp", axis=0, tiled=True)
    width_in = block_in.shape[0]
    shard_count = width_in // shard_width
    partials = jnp.einsum(
        "jot,joi->jit",
        block_in.reshape(shard_count, shard_width, col_count),
        weight_rows.reshape(shard_count, shard_width, shard_width),
        preferred_element_type=jnp.float32,
    )
    rounded = lax.optimization_barrier(partials.astype(jnp.bfloat16))
    grad_hidden = jnp.sum(rounded.astype(jnp.float32), axis=0)
    sigmoid_h = jax.nn.sigmoid(hidden)
    grad_pre = (grad_hidden * sigmoid_h * (1.0 + hidden * (1.0 - sigmoid_h))).astype(jnp.bfloat16)
    conv_grad = jnp.stack(
        [group_grad(tap_values, grad_pre) for tap_values in tap_set], axis=1
    ).reshape(groups_here, 3 * CG * CG)
    moved = grad_taps(grad_pre, shift_by)
    grad_input = (
        grad_out.astype(jnp.float32)
        + group_back(moved[0], tap_weights(conv_weight, 0))
        + group_back(moved[1], tap_weights(conv_weight, 1))
        + group_back(moved[2], tap_weights(conv_weight, 2))
    )
    summed = lax.psum((conv_grad, point_grad), "seq")
    conv_result = (summed[0] * gradient_scale).astype(jnp.bfloat16)
    point_result = (summed[1] * gradient_scale).astype(jnp.bfloat16)
    return (grad_input.astype(jnp.bfloat16), conv_result, point_result)


def local(
    embeddings,
    hilbert_order,
    cotangent,
    first_conv_weight,
    first_pointwise_weight,
    second_conv_weight,
    second_pointwise_weight,
):
    seq_count = lax.axis_size("seq")
    gradient_scale = float(embeddings.shape[1] * seq_count) ** (-0.5)
    near_shift = seq_count // 16
    far_shift = seq_count // 8
    local_index = hilbert_order - lax.axis_index("seq") * hilbert_order.shape[0]
    initial_token_rows = jnp.take(embeddings, local_index, axis=1)
    first_tap_rows, first_hidden_state, near_full = block_forward_step(
        initial_token_rows, first_conv_weight, near_shift
    )
    middle_rows = (
        initial_token_rows.astype(jnp.float32)
        + jnp.dot(first_pointwise_weight, near_full, preferred_element_type=jnp.float32)
    ).astype(jnp.bfloat16)
    second_tap_rows, second_hidden_state, far_full = block_forward_step(
        middle_rows, second_conv_weight, far_shift
    )
    middle_gradient, second_conv_gradient, second_pointwise_gradient = block_backward_step(
        cotangent,
        second_tap_rows,
        second_hidden_state,
        far_full,
        second_conv_weight,
        second_pointwise_weight,
        far_shift,
        gradient_scale,
    )
    start_gradient, first_conv_gradient, first_pointwise_gradient = block_backward_step(
        middle_gradient,
        first_tap_rows,
        first_hidden_state,
        near_full,
        first_conv_weight,
        first_pointwise_weight,
        near_shift,
        gradient_scale,
    )
    emb_grad = jnp.zeros_like(start_gradient).at[:, local_index].set(start_gradient)
    return (
        emb_grad,
        first_conv_gradient,
        first_pointwise_gradient,
        second_conv_gradient,
        second_pointwise_gradient,
    )


def solution(mesh):
    placed = (
        P("grp", "seq"),
        P("seq"),
        P("grp", "seq"),
        P("grp", None),
        P("grp", None),
        P("grp", None),
        P("grp", None),
    )
    return jax.shard_map(
        local,
        mesh=mesh,
        in_specs=placed,
        out_specs=(P("grp", "seq"), P("grp", None), P("grp", None), P("grp", None), P("grp", None)),
        check_vma=False,
    )
```

profile of v0, /device:TPU:1, one launch (start us, length us, event | category | flops | bytes accessed | tf_op | source)
XLA Modules:
  0.0 842.4 jit_solution(17735297071518127190)
XLA Ops:
  9.8 2.0 gather_fusion
  13.2 5.7 collective-permute-start
  20.7 1.6 collective-permute-done.1
  24.8 9.1 %all-to-all-start = ((bf16[192,8,192]{0,2,1:T(8,128)(2,1)}), bf16[192,8,192]{0,2,1:T(8,128)(2,1)S(1)}, u32[]{:S(2)}, u32[]{:S(2)}) async-start(bf16[192,8,192]{0,2,1:T(8,128)(2,1)} %bitcast), calls=%async_computation | async-start | bytes 1572864 | tf_op jit(solution)/shard_map/all_to_all | solution.py:85
  35.5 15.1 %all-to-all-done = bf16[192,8,192]{0,2,1:T(8,128)(2,1)S(1)} async-done(((bf16[192,8,192]{0,2,1:T(8,128)(2,1)}), bf16[192,8,192]{0,2,1:T(8,128)(2,1)S(1)}, u32[]{:S(2)}, u32[]{:S(2)}) %all-to-all-start) | async-done | bytes 589856 | tf_op jit(solution)/shard_map/all_to_all | solution.py:85
  50.7 21.0 %all-gather.5.cloned.1.call-done = bf16[1536,512]{1,0:T(8,128)(2,1)} async-done(((bf16[192,512]{1,0:T(8,128)(2,1)}), bf16[1536,512]{1,0:T(8,128)(2,1)}) %all-gather.5.cloned.1.call-update) | async-done | bytes 1572880 | tf_op jit(solution)/shard_map/all_gather | solution.py:86
  71.6 2.0 convolution_convert_fusion.1
  73.9 49.9 %all-gather.7.cloned.1.call-done = bf16[1536,512]{1,0:T(8,128)(2,1)} async-done(((bf16[192,512]{1,0:T(8,128)(2,1)}), bf16[1536,512]{1,0:T(8,128)(2,1)}) %all-gather.7.cloned.1.call-update) | async-done | bytes 1572880 | tf_op jit(solution)/shard_map/all_gather | solution.py:73
  123.7 1.9 fusion.12
  126.9 7.9 collective-permute-start.2
  139.9 15.3 %collective-permute-start.5 = (bf16[192,512]{1,0:T(8,128)(2,1)S(1)}, bf16[192,512]{1,0:T(8,128)(2,1)S(1)}, u32[]{:S(2)}, u32[]{:S(2)}) collective-permute-start(bf16[192,512]{1,0:T(8,128)(2,1)S(1)} %get-tuple-element.17), channel_id=1, source_target_pairs={{0,64},{8,72},{16,80},{24,88},{32,96},{40,104},{48,112},{56,120},{... | collective-permute-start | bytes 589832 | tf_op jit(solution)/shard_map/ppermute | solution.py:12
  156.6 3.6 collective-permute-done.5
  162.3 3.7 all-to-all-start.1
  168.1 1.7 fusion.27
  169.9 39.5 %all-gather.11.cloned.1.call-done = bf16[1536,512]{1,0:T(8,128)(2,1)} async-done(((bf16[192,512]{1,0:T(8,128)(2,1)}), bf16[1536,512]{1,0:T(8,128)(2,1)}) %all-gather.11.cloned.1.call-update) | async-done | bytes 1572880 | tf_op jit(solution)/shard_map/all_gather | solution.py:73
  209.4 3.1 convolution_bitcast_fusion
  212.5 49.4 %all-gather.9.cloned.1.call-done = bf16[1536,512]{1,0:T(8,128)(2,1)} async-done(((bf16[192,512]{1,0:T(8,128)(2,1)}), bf16[1536,512]{1,0:T(8,128)(2,1)}) %all-gather.9.cloned.1.call-update) | async-done | bytes 1572880 | tf_op jit(solution)/shard_map/all_gather | solution.py:86
  261.9 2.0 fusion
  267.1 4.2 collective-permute-start.7
  273.0 13.5 %collective-permute-done.6 = bf16[192,512]{1,0:T(8,128)(2,1)S(1)} collective-permute-done((bf16[192,512]{1,0:T(8,128)(2,1)S(1)}, bf16[192,512]{1,0:T(8,128)(2,1)S(1)}, u32[]{:S(2)}, u32[]{:S(2)}) %collective-permute-start.6) | collective-permute-done | bytes 196640 | tf_op jit(solution)/shard_map/ppermute | solution.py:12
  287.0 2.4 scatter_custom_fusion
  290.2 540.1 %all-reduce.3.cloned.1.call-done = (f32[1,110592]{1,0:T(1,128)}, f32[192,1536]{1,0:T(8,128)}, f32[1,110592]{1,0:T(1,128)}, f32[192,1536]{1,0:T(8,128)}) async-done(((f32[1,110592]{1,0:T(1,128)}, f32[192,1536]{1,0:T(8,128)}, f32[1,110592]{1,0:T(1,128)}, f32[192,1536]{1,0:T(8,128)}), (f32[1,110592]{1,0:T(1,128)}, f32[192,1536]{1,0:T(8,128)}, f32[1,110592]{1,0:T(1,128)}, ...) | async-done | bytes 3244048 | tf_op jit(solution)/shard_map/psum | solution.py:109
  830.3 3.1 multiply_convert_fusion.2
  833.3 2.5 multiply_convert_fusion
  (98 shorter events, 28.1 us)
Async XLA Ops:
  7.2 64.5 %all-gather.5.cloned.1.call-start = ((), (), s32[]{:S(2)}) async-start(), calls=%async_computation.2 | async-start | bytes 1769472 | tf_op jit(solution)/shard_map/all_gather | solution.py:86
  7.9 11.0 %copy-start.13 = (bf16[1,110592]{1,0:T(2,128)(2,1)S(1)}, bf16[1,110592]{1,0:T(2,128)(2,1)}, u32[]{:S(2)}) copy-start(bf16[1,110592]{1,0:T(2,128)(2,1)} %param.10) | copy-start | bytes 663556
  7.9 115.8 %all-gather.7.cloned.1.call-start = ((), (), s32[]{:S(2)}) async-start(), calls=%async_computation.3 | async-start | bytes 1769472 | tf_op jit(solution)/shard_map/all_gather | solution.py:73
  11.9 10.4 %collective-permute-start.1 = (bf16[192,512]{1,0:T(8,128)(2,1)S(1)}, bf16[192,512]{1,0:T(8,128)(2,1)S(1)}, u32[]{:S(2)}, u32[]{:S(2)}) collective-permute-start(bf16[192,512]{1,0:T(8,128)(2,1)S(1)} %fusion.17), channel_id=1, source_target_pairs={{32,0},{40,8},{48,16},{56,24},{64,32},{72,40},{80,48},{88,56},{96,... | collective-permute-start | bytes 589832 | tf_op jit(solution)/shard_map/ppermute | solution.py:12
  13.2 9.3 %collective-permute-start = (bf16[192,512]{1,0:T(8,128)(2,1)S(1)}, bf16[192,512]{1,0:T(8,128)(2,1)S(1)}, u32[]{:S(2)}, u32[]{:S(2)}) collective-permute-start(bf16[192,512]{1,0:T(8,128)(2,1)S(1)} %fusion.17), channel_id=1, source_target_pairs={{0,32},{8,40},{16,48},{24,56},{32,64},{40,72},{48,80},{56,88},{64,... | collective-permute-start | bytes 589832 | tf_op jit(solution)/shard_map/ppermute | solution.py:12
  20.4 3.3 copy-start.3
  23.7 10.3 %copy-start.14 = (bf16[1,110592]{1,0:T(2,128)(2,1)S(1)}, bf16[1,110592]{1,0:T(2,128)(2,1)}, u32[]{:S(2)}) copy-start(bf16[1,110592]{1,0:T(2,128)(2,1)} %param.12) | copy-start | bytes 663556
  24.8 25.8 %all-to-all-start = ((bf16[192,8,192]{0,2,1:T(8,128)(2,1)}), bf16[192,8,192]{0,2,1:T(8,128)(2,1)S(1)}, u32[]{:S(2)}, u32[]{:S(2)}) async-start(bf16[192,8,192]{0,2,1:T(8,128)(2,1)} %bitcast), calls=%async_computation | async-start | bytes 1572864 | tf_op jit(solution)/shard_map/all_to_all | solution.py:85
  33.9 175.5 %all-gather.11.cloned.1.call-start = ((), (), s32[]{:S(2)}) async-start(), calls=%async_computation.5 | async-start | bytes 1769472 | tf_op jit(solution)/shard_map/all_gather | solution.py:73
  73.6 50.1 %copy-start.2 = (bf16[192,1536]{1,0:T(8,128)(2,1)S(1)}, bf16[192,1536]{1,0:T(8,128)(2,1)}, u32[]{:S(2)}) copy-start(bf16[192,1536]{1,0:T(8,128)(2,1)} %param.11) | copy-start | bytes 1769476
  125.6 10.9 %collective-permute-start.3 = (bf16[192,512]{1,0:T(8,128)(2,1)S(1)}, bf16[192,512]{1,0:T(8,128)(2,1)S(1)}, u32[]{:S(2)}, u32[]{:S(2)}) collective-permute-start(bf16[192,512]{1,0:T(8,128)(2,1)S(1)} %fusion.12), channel_id=1, source_target_pairs={{64,0},{72,8},{80,16},{88,24},{96,32},{104,40},{112,48},{120,56},{... | collective-permute-start | bytes 589832 | tf_op jit(solution)/shard_map/ppermute | solution.py:12
  126.9 10.5 %collective-permute-start.2 = (bf16[192,512]{1,0:T(8,128)(2,1)S(1)}, bf16[192,512]{1,0:T(8,128)(2,1)S(1)}, u32[]{:S(2)}, u32[]{:S(2)}) collective-permute-start(bf16[192,512]{1,0:T(8,128)(2,1)S(1)} %fusion.12), channel_id=1, source_target_pairs={{0,64},{8,72},{16,80},{24,88},{32,96},{40,104},{48,112},{56,120},{... | collective-permute-start | bytes 589832 | tf_op jit(solution)/shard_map/ppermute | solution.py:12
  137.2 19.2 %copy-start.5 = (bf16[192,512]{1,0:T(8,128)(2,1)S(1)}, bf16[192,512]{1,0:T(8,128)(2,1)}, u32[]{:S(2)}) copy-start(bf16[192,512]{1,0:T(8,128)(2,1)} %param.9) | copy-start | bytes 589828
  138.5 123.3 %all-gather.9.cloned.1.call-start = ((), (), s32[]{:S(2)}) async-start(), calls=%async_computation.4 | async-start | bytes 1769472 | tf_op jit(solution)/shard_map/all_gather | solution.py:86
  138.6 17.8 %collective-permute-start.4 = (bf16[192,512]{1,0:T(8,128)(2,1)S(1)}, bf16[192,512]{1,0:T(8,128)(2,1)S(1)}, u32[]{:S(2)}, u32[]{:S(2)}) collective-permute-start(bf16[192,512]{1,0:T(8,128)(2,1)S(1)} %get-tuple-element.17), channel_id=1, source_target_pairs={{64,0},{72,8},{80,16},{88,24},{96,32},{104,40},{112,48},{120,56},{... | collective-permute-start | bytes 589832 | tf_op jit(solution)/shard_map/ppermute | solution.py:12
  139.9 20.3 %collective-permute-start.5 = (bf16[192,512]{1,0:T(8,128)(2,1)S(1)}, bf16[192,512]{1,0:T(8,128)(2,1)S(1)}, u32[]{:S(2)}, u32[]{:S(2)}) collective-permute-start(bf16[192,512]{1,0:T(8,128)(2,1)S(1)} %get-tuple-element.17), channel_id=1, source_target_pairs={{0,64},{8,72},{16,80},{24,88},{32,96},{40,104},{48,112},{56,120},{... | collective-permute-start | bytes 589832 | tf_op jit(solution)/shard_map/ppermute | solution.py:12
  162.3 4.0 copy-start.11
  162.3 4.2 copy-start.19
  162.3 50.2 %all-to-all-start.1 = ((bf16[192,8,192]{0,2,1:T(8,128)(2,1)}), bf16[192,8,192]{0,2,1:T(8,128)(2,1)S(1)}, u32[]{:S(2)}, u32[]{:S(2)}) async-start(bf16[192,8,192]{0,2,1:T(8,128)(2,1)} %bitcast.17), calls=%async_computation.1 | async-start | bytes 1572864 | tf_op jit(solution)/shard_map/all_to_all | solution.py:85
  166.0 664.3 %all-reduce.3.cloned.1.call-start = ((), (), s32[]{:S(2)}) async-start(), calls=%async_computation.6 | async-start | bytes 6488064 | tf_op jit(solution)/shard_map/psum | solution.py:109
  168.1 41.3 %copy-start.6 = (bf16[192,512]{1,0:T(8,128)(2,1)S(1)}, bf16[192,512]{1,0:T(8,128)(2,1)}, u32[]{:S(2)}) copy-start(bf16[192,512]{1,0:T(8,128)(2,1)} %param.9) | copy-start | bytes 589828
  267.1 5.7 copy-start.4
  267.1 19.5 %collective-permute-start.7 = (bf16[192,512]{1,0:T(8,128)(2,1)S(1)}, bf16[192,512]{1,0:T(8,128)(2,1)S(1)}, u32[]{:S(2)}, u32[]{:S(2)}) collective-permute-start(bf16[192,512]{1,0:T(8,128)(2,1)S(1)} %multiply_convert_fusion.5), channel_id=1, source_target_pairs={{0,32},{8,40},{16,48},{24,56},{32,64},{40,72},{48,80},{56,88},{64,... | collective-permute-start | bytes 589832 | tf_op jit(solution)/shard_map/ppermute | solution.py:12
  271.3 15.1 %collective-permute-start.6 = (bf16[192,512]{1,0:T(8,128)(2,1)S(1)}, bf16[192,512]{1,0:T(8,128)(2,1)S(1)}, u32[]{:S(2)}, u32[]{:S(2)}) collective-permute-start(bf16[192,512]{1,0:T(8,128)(2,1)S(1)} %multiply_convert_fusion.5), channel_id=1, source_target_pairs={{32,0},{40,8},{48,16},{56,24},{64,32},{72,40},{80,48},{88,56},{96,... | collective-permute-start | bytes 589832 | tf_op jit(solution)/shard_map/ppermute | solution.py:12
  (11 other events, 19.1 us)
Sparse Core Ops, SparseCore 0:
  10.1 61.5 all-gather.4
  74.3 49.3 all-gather.6
  138.6 70.7 all-gather.10
  211.9 49.9 all-gather.8
  267.2 562.9 all-reduce.2
where the time goes:
time: 843 us; the launch traced here: 842 us
  waiting for transfers between devices  737 us (87%)
  starting transfers between devices  51.4 us (6%)
  matrix products  17 us (2%)
  between operations  14.2 us (2%)
  local copies, waits for them, and re-layouts  13.1 us (2%)
  other arithmetic  9.59 us (1%)
    psum x1, waiting for transfers between devices, block_backward_step(): summed = lax.psum((conv_grad, point_grad), 'seq')  540 us
    all_gather x2, waiting for transfers between devices, block_forward_step(): gathered = lax.all_gather(activated, 'grp', axis=0, tiled=True)  89.4 us
    all_gather x2, waiting for transfers between devices, block_backward_step(): block_in = lax.all_gather(grad_out, 'grp', axis=0, tiled=True)  70.3 us
    ppermute x8, starting transfers between devices, passed_along(): return lax.ppermute(block, axis, route)  38.4 us
    ppermute x8, waiting for transfers between devices, passed_along(): return lax.ppermute(block, axis, route)  21.3 us
  transfers between devices with their start and end apart: 15, of which 12 were waited for; matrix products, arithmetic and copies ran while one was open for 3% of the time, Pallas kernels for 0%

commit v1 on v0

--- a/solution.py
+++ b/solution.py
@@ -70,7 +70,9 @@
         + group_apply(tap_set[2], tap_weights(conv_weight, 2))
     )
     activated = jax.nn.silu(hidden).astype(jnp.bfloat16)
-    gathered = lax.all_gather(activated, "grp", axis=0, tiled=True)
+    gathered = jnp.concatenate(
+        lax.all_to_all(jnp.stack([activated] * lax.axis_size("grp")), "grp", 0, 0), axis=0
+    )
     return (tap_set, hidden, gathered)
 
 

time: 843 us -> 793 us (0.941)
  waiting for transfers between devices: 737 us -> 661 us
  starting transfers between devices: 51.4 us -> 67 us
    all_gather x2 -> x0, waiting for transfers between devices: 89.4 us -> none  [block_forward_step(): gathered = lax.all_gather(activated, 'grp', axis=0, tiled=True)]
    all_to_all x0 -> x2, starting transfers between devices: none -> 17 us  [block_forward_step(): lax.all_to_all(jnp.stack([activated] * lax.axis_size('grp')), 'grp', 0, 0)]
    all_to_all x2, waiting for transfers between devices: 15.1 us -> 0.95 us  [block_backward_step(): lax.all_to_all(pointwise, 'grp', split_axis=1, concat_axis=0, tiled=True)]
    all_gather x2, waiting for transfers between devices: 70.3 us -> 83.5 us  [block_backward_step(): block_in = lax.all_gather(grad_out, 'grp', axis=0, tiled=True)]
    ppermute x8, waiting for transfers between devices: 21.3 us -> 33.7 us  [passed_along(): return lax.ppermute(block, axis, route)]
  transfers between devices with their start and end apart: 15 -> 15, of which waited for: 12 -> 9; matrix products, arithmetic and copies ran while one was open for 3% -> 4% of each run, Pallas kernels for 0% -> 0%
where the time goes in v1:
time: 793 us; the launch traced here: 791 us
  waiting for transfers between devices  661 us (83%)
  starting transfers between devices  67 us (8%)
  matrix products  19.5 us (2%)
  local copies, waits for them, and re-layouts  18.3 us (2%)
  between operations  14.2 us (2%)
  other arithmetic  11.4 us (1%)
    psum x1, waiting for transfers between devices, block_backward_step(): summed = lax.psum((conv_grad, point_grad), 'seq')  543 us
    all_gather x2, waiting for transfers between devices, block_backward_step(): block_in = lax.all_gather(grad_out, 'grp', axis=0, tiled=True)  83.5 us
    ppermute x8, starting transfers between devices, passed_along(): return lax.ppermute(block, axis, route)  36.6 us
    ppermute x8, waiting for transfers between devices, passed_along(): return lax.ppermute(block, axis, route)  33.7 us
    all_to_all x2, starting transfers between devices, block_forward_step(): lax.all_to_all(jnp.stack([activated] * lax.axis_size('grp')), 'grp', 0, 0)  17 us
  transfers between devices with their start and end apart: 15, of which 9 were waited for; matrix products, arithmetic and copies ran while one was open for 4% of the time, Pallas kernels for 0%

profile of v1, /device:TPU:1, one launch (start us, length us, event | category | flops | bytes accessed | tf_op | source)
XLA Modules:
  0.0 791.5 jit_solution(9601181794721546733)
XLA Ops:
  7.2 2.3 copy.12
  9.5 6.6 all-to-all-start
  16.4 2.0 gather_fusion
  19.8 4.9 collective-permute-start
  26.5 3.1 collective-permute-done.1
  32.2 3.6 all-to-all-start.1
  35.8 2.2 reduce
  38.3 49.1 %all-gather.3.cloned.1.call-done = bf16[1536,512]{1,0:T(8,128)(2,1)} async-done(((bf16[192,512]{1,0:T(8,128)(2,1)}), bf16[1536,512]{1,0:T(8,128)(2,1)}) %all-gather.3.cloned.1.call-update) | async-done | bytes 1572880 | tf_op jit(solution)/shard_map/all_gather | solution.py:88
  87.3 2.0 convolution_convert_fusion.1
  92.2 13.6 %collective-permute-start.2 = (bf16[192,512]{1,0:T(8,128)(2,1)S(1)}, bf16[192,512]{1,0:T(8,128)(2,1)S(1)}, u32[]{:S(2)}, u32[]{:S(2)}) collective-permute-start(bf16[192,512]{1,0:T(8,128)(2,1)S(1)} %fusion.12), channel_id=1, source_target_pairs={{0,64},{8,72},{16,80},{24,88},{32,96},{40,104},{48,112},{56,120},{... | collective-permute-start | bytes 589832 | tf_op jit(solution)/shard_map/ppermute | solution.py:12
  110.6 13.4 %all-to-all-start.3 = ((bf16[8,192,512]{2,1,0:T(8,128)(2,1)}), bf16[8,192,512]{2,1,0:T(8,128)(2,1)S(1)}, u32[]{:S(2)}, u32[]{:S(2)}) async-start(bf16[8,192,512]{2,1,0:T(8,128)(2,1)} %stack.55), calls=%async_computation.3 | async-start | bytes 3145728 | tf_op jit(solution)/shard_map/all_to_all | solution.py:74
  124.0 8.8 %collective-permute-start.5 = (bf16[192,512]{1,0:T(8,128)(2,1)S(1)}, bf16[192,512]{1,0:T(8,128)(2,1)S(1)}, u32[]{:S(2)}, u32[]{:S(2)}) collective-permute-start(bf16[192,512]{1,0:T(8,128)(2,1)S(1)} %get-tuple-element.17), channel_id=1, source_target_pairs={{0,64},{8,72},{16,80},{24,88},{32,96},{40,104},{48,112},{56,120},{... | collective-permute-start | bytes 589832 | tf_op jit(solution)/shard_map/ppermute | solution.py:12
  135.2 13.6 %collective-permute-done.4 = bf16[192,512]{1,0:T(8,128)(2,1)S(1)} collective-permute-done((bf16[192,512]{1,0:T(8,128)(2,1)S(1)}, bf16[192,512]{1,0:T(8,128)(2,1)S(1)}, u32[]{:S(2)}, u32[]{:S(2)}) %collective-permute-start.4) | collective-permute-done | bytes 196640 | tf_op jit(solution)/shard_map/ppermute | solution.py:12
  151.8 2.3 copy.15
  154.1 6.5 all-to-all-start.2
  165.4 2.4 reshape.246
  172.1 34.4 %all-gather.5.cloned.1.call-done = bf16[1536,512]{1,0:T(8,128)(2,1)} async-done(((bf16[192,512]{1,0:T(8,128)(2,1)}), bf16[1536,512]{1,0:T(8,128)(2,1)}) %all-gather.5.cloned.1.call-update) | async-done | bytes 1572880 | tf_op jit(solution)/shard_map/all_gather | solution.py:88
  206.5 2.2 fusion
  212.0 4.2 collective-permute-start.7
  217.7 15.1 %collective-permute-done.6 = bf16[192,512]{1,0:T(8,128)(2,1)S(1)} collective-permute-done((bf16[192,512]{1,0:T(8,128)(2,1)S(1)}, bf16[192,512]{1,0:T(8,128)(2,1)S(1)}, u32[]{:S(2)}, u32[]{:S(2)}) %collective-permute-start.6) | collective-permute-done | bytes 196640 | tf_op jit(solution)/shard_map/ppermute | solution.py:12
  233.4 2.4 scatter_custom_fusion
  236.6 542.8 %all-reduce.3.cloned.1.call-done = (f32[1,110592]{1,0:T(1,128)}, f32[192,1536]{1,0:T(8,128)}, f32[1,110592]{1,0:T(1,128)}, f32[192,1536]{1,0:T(8,128)}) async-done(((f32[1,110592]{1,0:T(1,128)}, f32[192,1536]{1,0:T(8,128)}, f32[1,110592]{1,0:T(1,128)}, f32[192,1536]{1,0:T(8,128)}), (f32[1,110592]{1,0:T(1,128)}, f32[192,1536]{1,0:T(8,128)}, f32[1,110592]{1,0:T(1,128)}, ...) | async-done | bytes 3244048 | tf_op jit(solution)/shard_map/psum | solution.py:111
  779.4 3.1 multiply_convert_fusion.2
  782.5 2.5 multiply_convert_fusion
  (98 shorter events, 34.3 us)
Async XLA Ops:
  7.2 9.0 %copy-start.19 = (s32[512]{0:T(512)S(1)}, s32[512]{0:T(512)}, u32[]{:S(2)}) copy-start(s32[512]{0:T(512)} %param.8) | copy-start | bytes 6148
  7.2 9.0 %copy-start.15 = (bf16[192,512]{1,0:T(8,128)(2,1)S(1)}, bf16[192,512]{1,0:T(8,128)(2,1)}, u32[]{:S(2)}) copy-start(bf16[192,512]{1,0:T(8,128)(2,1)} %param.7) | copy-start | bytes 589828
  9.5 21.5 %all-to-all-start = ((bf16[192,8,192]{0,2,1:T(8,128)(2,1)}), bf16[192,8,192]{0,2,1:T(8,128)(2,1)S(1)}, u32[]{:S(2)}, u32[]{:S(2)}) async-start(bf16[192,8,192]{0,2,1:T(8,128)(2,1)} %bitcast), calls=%async_computation | async-start | bytes 1572864 | tf_op jit(solution)/shard_map/all_to_all | solution.py:87
  16.1 71.2 %all-gather.3.cloned.1.call-start = ((), (), s32[]{:S(2)}) async-start(), calls=%async_computation.4 | async-start | bytes 1769472 | tf_op jit(solution)/shard_map/all_gather | solution.py:88
  16.2 8.5 %copy-start.12 = (bf16[1,110592]{1,0:T(2,128)(2,1)S(1)}, bf16[1,110592]{1,0:T(2,128)(2,1)}, u32[]{:S(2)}) copy-start(bf16[1,110592]{1,0:T(2,128)(2,1)} %param.10) | copy-start | bytes 663556
  18.5 11.1 %collective-permute-start.1 = (bf16[192,512]{1,0:T(8,128)(2,1)S(1)}, bf16[192,512]{1,0:T(8,128)(2,1)S(1)}, u32[]{:S(2)}, u32[]{:S(2)}) collective-permute-start(bf16[192,512]{1,0:T(8,128)(2,1)S(1)} %fusion.17), channel_id=1, source_target_pairs={{32,0},{40,8},{48,16},{56,24},{64,32},{72,40},{80,48},{88,56},{96,... | collective-permute-start | bytes 589832 | tf_op jit(solution)/shard_map/ppermute | solution.py:12
  19.8 10.1 %collective-permute-start = (bf16[192,512]{1,0:T(8,128)(2,1)S(1)}, bf16[192,512]{1,0:T(8,128)(2,1)S(1)}, u32[]{:S(2)}, u32[]{:S(2)}) collective-permute-start(bf16[192,512]{1,0:T(8,128)(2,1)S(1)} %fusion.17), channel_id=1, source_target_pairs={{0,32},{8,40},{16,48},{24,56},{32,64},{40,72},{48,80},{56,88},{64,... | collective-permute-start | bytes 589832 | tf_op jit(solution)/shard_map/ppermute | solution.py:12
  32.2 58.1 %all-to-all-start.1 = ((bf16[8,192,512]{2,1,0:T(8,128)(2,1)}), bf16[8,192,512]{2,1,0:T(8,128)(2,1)S(1)}, u32[]{:S(2)}, u32[]{:S(2)}) async-start(bf16[8,192,512]{2,1,0:T(8,128)(2,1)} %stack.20), calls=%async_computation.1 | async-start | bytes 3145728 | tf_op jit(solution)/shard_map/all_to_all | solution.py:74
  38.2 70.4 %copy-start.5 = (bf16[1,3,192,192]{3,2,1,0:T(8,128)(2,1)}, bf16[1,3,192,192]{3,2,1,0:T(8,128)(2,1)S(1)}, u32[]{:S(2)}) copy-start(bf16[1,3,192,192]{3,2,1,0:T(8,128)(2,1)S(1)} %reshape.240) | copy-start | bytes 663556
  90.4 18.2 %copy-start.14 = (f32[192,512]{1,0:T(8,128)S(1)}, f32[192,512]{1,0:T(8,128)}, u32[]{:S(2)}) copy-start(f32[192,512]{1,0:T(8,128)} %convert_reduce_fusion.1) | copy-start | bytes 1179652
  90.8 18.2 %copy-start.7 = (bf16[192,512]{1,0:T(8,128)(2,1)}, bf16[192,512]{1,0:T(8,128)(2,1)S(1)}, u32[]{:S(2)}) copy-start(bf16[192,512]{1,0:T(8,128)(2,1)S(1)} %fusion.12) | copy-start | bytes 589828
  90.9 17.0 %collective-permute-start.3 = (bf16[192,512]{1,0:T(8,128)(2,1)S(1)}, bf16[192,512]{1,0:T(8,128)(2,1)S(1)}, u32[]{:S(2)}, u32[]{:S(2)}) collective-permute-start(bf16[192,512]{1,0:T(8,128)(2,1)S(1)} %fusion.12), channel_id=1, source_target_pairs={{64,0},{72,8},{80,16},{88,24},{96,32},{104,40},{112,48},{120,56},{... | collective-permute-start | bytes 589832 | tf_op jit(solution)/shard_map/ppermute | solution.py:12
  92.2 16.4 %collective-permute-start.2 = (bf16[192,512]{1,0:T(8,128)(2,1)S(1)}, bf16[192,512]{1,0:T(8,128)(2,1)S(1)}, u32[]{:S(2)}, u32[]{:S(2)}) collective-permute-start(bf16[192,512]{1,0:T(8,128)(2,1)S(1)} %fusion.12), channel_id=1, source_target_pairs={{0,64},{8,72},{16,80},{24,88},{32,96},{40,104},{48,112},{56,120},{... | collective-permute-start | bytes 589832 | tf_op jit(solution)/shard_map/ppermute | solution.py:12
  109.3 51.5 %copy-start.1 = (bf16[192,512]{1,0:T(8,128)(2,1)}, bf16[192,512]{1,0:T(8,128)(2,1)S(1)}, u32[]{:S(2)}) copy-start(bf16[192,512]{1,0:T(8,128)(2,1)S(1)} %get-tuple-element.17) | copy-start | bytes 589828
  110.6 43.5 %all-to-all-start.3 = ((bf16[8,192,512]{2,1,0:T(8,128)(2,1)}), bf16[8,192,512]{2,1,0:T(8,128)(2,1)S(1)}, u32[]{:S(2)}, u32[]{:S(2)}) async-start(bf16[8,192,512]{2,1,0:T(8,128)(2,1)} %stack.55), calls=%async_computation.3 | async-start | bytes 3145728 | tf_op jit(solution)/shard_map/all_to_all | solution.py:74
  124.0 82.5 %all-gather.5.cloned.1.call-start = ((), (), s32[]{:S(2)}) async-start(), calls=%async_computation.5 | async-start | bytes 1769472 | tf_op jit(solution)/shard_map/all_gather | solution.py:88
  124.0 26.0 %collective-permute-start.5 = (bf16[192,512]{1,0:T(8,128)(2,1)S(1)}, bf16[192,512]{1,0:T(8,128)(2,1)S(1)}, u32[]{:S(2)}, u32[]{:S(2)}) collective-permute-start(bf16[192,512]{1,0:T(8,128)(2,1)S(1)} %get-tuple-element.17), channel_id=1, source_target_pairs={{0,64},{8,72},{16,80},{24,88},{32,96},{40,104},{48,112},{56,120},{... | collective-permute-start | bytes 589832 | tf_op jit(solution)/shard_map/ppermute | solution.py:12
  132.8 16.0 %collective-permute-start.4 = (bf16[192,512]{1,0:T(8,128)(2,1)S(1)}, bf16[192,512]{1,0:T(8,128)(2,1)S(1)}, u32[]{:S(2)}, u32[]{:S(2)}) collective-permute-start(bf16[192,512]{1,0:T(8,128)(2,1)S(1)} %get-tuple-element.17), channel_id=1, source_target_pairs={{64,0},{72,8},{80,16},{88,24},{96,32},{104,40},{112,48},{120,56},{... | collective-permute-start | bytes 589832 | tf_op jit(solution)/shard_map/ppermute | solution.py:12
  154.1 18.0 %all-to-all-start.2 = ((bf16[192,8,192]{0,2,1:T(8,128)(2,1)}), bf16[192,8,192]{0,2,1:T(8,128)(2,1)}, u32[]{:S(2)}, u32[]{:S(2)}) async-start(bf16[192,8,192]{0,2,1:T(8,128)(2,1)} %bitcast.134), calls=%async_computation.2 | async-start | bytes 1572864 | tf_op jit(solution)/shard_map/all_to_all | solution.py:87
  160.5 618.9 %all-reduce.3.cloned.1.call-start = ((), (), s32[]{:S(2)}) async-start(), calls=%async_computation.6 | async-start | bytes 6488064 | tf_op jit(solution)/shard_map/psum | solution.py:111
  161.9 5.8 copy-start
  212.0 5.5 copy-start.4
  212.0 21.0 %collective-permute-start.7 = (bf16[192,512]{1,0:T(8,128)(2,1)S(1)}, bf16[192,512]{1,0:T(8,128)(2,1)S(1)}, u32[]{:S(2)}, u32[]{:S(2)}) collective-permute-start(bf16[192,512]{1,0:T(8,128)(2,1)S(1)} %multiply_convert_fusion.5), channel_id=1, source_target_pairs={{0,32},{8,40},{16,48},{24,56},{32,64},{40,72},{48,80},{56,88},{64,... | collective-permute-start | bytes 589832 | tf_op jit(solution)/shard_map/ppermute | solution.py:12
  216.2 16.6 %collective-permute-start.6 = (bf16[192,512]{1,0:T(8,128)(2,1)S(1)}, bf16[192,512]{1,0:T(8,128)(2,1)S(1)}, u32[]{:S(2)}, u32[]{:S(2)}) collective-permute-start(bf16[192,512]{1,0:T(8,128)(2,1)S(1)} %multiply_convert_fusion.5), channel_id=1, source_target_pairs={{32,0},{40,8},{48,16},{56,24},{64,32},{72,40},{80,48},{88,56},{96,... | collective-permute-start | bytes 589832 | tf_op jit(solution)/shard_map/ppermute | solution.py:12
  (11 other events, 20.6 us)
Sparse Core Ops, SparseCore 0:
  24.8 62.4 all-gather.2
  151.9 54.5 all-gather.4
  212.1 567.2 all-reduce.2
